TPU v7x, 32 devices: a whole 2x2x4 slice. The times are simulated.
32 devices in a mesh: energy: 16 (over z, y, x), space: 2 (over core).
Axes of the slice: x: 2, y: 2, z: 4, core: 2. Of those that a mesh axis runs over, the one named last changes fastest.
Arguments:
- lesser: bfloat16 [32, 2, 2, 384, 384], P('energy', 'space'), may hold values from -6 to 6
- coupling: bfloat16 [2, 2, 384, 384], P('space'), may hold values from -0.21875 to 0.21875
- neighbours: int32 [2, 3], P('space'), may hold values from 0 to 1, as said below
- greater: bfloat16 [32, 2, 2, 384, 384], P(None, 'space', None, 'energy'), may hold values from -0.75 to 0.75
- closing: bfloat16 [2, 2, 384, 384], P('space'), may hold values from -0.21875 to 0.21875
Outputs:
- sigma: bfloat16 [32, 2, 2, 384, 384], P('energy', 'space')
Inputs may be any that keep to these rules, and one draw needn't show every extreme that they name: `neighbours`: row i names only blocks i - 1, i and i + 1, clipped to 0 .. 1; every row other than the first and the last names both i - 1 and i + 1.
All inputs are finite; a program needn't handle non-finite values.
Results may differ from a plain program's by a relative error of at most 0.007.
Values may be sent and summed in bfloat16 or wider, within the bound.
A program may use at most 64 MiB of HBM per device.

v0:
```python
import math

import jax
import jax.numpy as jnp
from jax import lax
from jax.sharding import PartitionSpec as P


def shifted(block, axis, distance):
    devices = range(lax.axis_size(axis))
    route = [(i - distance, i) for i in devices if i - distance in devices]
    return lax.ppermute(block, axis, route)


def left_product(left_real, left_imag, right_real, right_imag):

    def mult(a, b):
        return jnp.einsum("rs,est->ert", a, b, preferred_element_type=jnp.float32)

    real_part = mult(left_real, right_real) - mult(left_imag, right_imag)
    imag_part = mult(left_real, right_imag) + mult(left_imag, right_real)
    return (real_part.astype(jnp.bfloat16), imag_part.astype(jnp.bfloat16))


def right_adjoint(left_real, left_imag, right_real, right_imag):

    def mult(a, b):
        return jnp.einsum("ers,ts->ert", a, b, preferred_element_type=jnp.float32)

    real_part = mult(left_real, right_real) + mult(left_imag, right_imag)
    imag_part = mult(left_imag, right_real) - mult(left_real, right_imag)
    return (real_part, imag_part)


def exact_dot(table, values):
    return jnp.dot(
        table, values, precision=lax.Precision.HIGHEST, preferred_element_type=jnp.float32
    )


def convolve(regrouped, greater):
    points = regrouped.shape[0]
    blocks = regrouped.shape[1]
    rows_here = regrouped.shape[3]
    columns = regrouped.shape[4]
    freq = lax.broadcasted_iota(jnp.int32, (points, points), 0)
    spot = lax.broadcasted_iota(jnp.int32, (points, points), 1)
    phase = (freq * spot % points).astype(jnp.float32) * (2.0 * math.pi / points)
    cosine = jnp.cos(phase)
    sine = jnp.sin(phase)
    screened = greater.astype(jnp.float32)

    def forward(real_part, imag_part):
        real_flat = real_part.reshape(points, -1)
        imag_flat = imag_part.reshape(points, -1)
        return (
            exact_dot(cosine, real_flat) + exact_dot(sine, imag_flat),
            exact_dot(cosine, imag_flat) - exact_dot(sine, real_flat),
        )

    left_real, left_imag = forward(regrouped[:, :, 0], regrouped[:, :, 1])
    right_real, right_imag = forward(screened[:, :, 0], screened[:, :, 1])
    prod_real = left_real * right_real - left_imag * right_imag
    prod_imag = left_real * right_imag + left_imag * right_real
    back_real = (exact_dot(cosine, prod_real) - exact_dot(sine, prod_imag)) / points
    back_imag = (exact_dot(cosine, prod_imag) + exact_dot(sine, prod_real)) / points
    shape = (points, blocks, rows_here, columns)
    return jnp.stack([back_real.reshape(shape), back_imag.reshape(shape)], axis=2).astype(
        jnp.bfloat16
    )


def local(lesser, coupling, neighbours, greater, closing):
    blocks = lesser.shape[1]
    below = shifted(coupling, "space", 1)
    above = shifted(coupling, "space", -1)
    source = jnp.concatenate([below, coupling, above], axis=0)
    offset = lax.axis_index("space") * blocks - 1
    local_index = neighbours - offset
    column = 0
    energy_slab = lesser[:, column]
    total_real = jnp.zeros(energy_slab[:, 0].shape, jnp.float32)
    total_imag = jnp.zeros(energy_slab[:, 0].shape, jnp.float32)
    for term in range(3):
        matrix = lax.dynamic_index_in_dim(source, local_index[column, term], 0, keepdims=False)
        part_real, part_imag = left_product(
            matrix[0], matrix[1], energy_slab[:, 0], energy_slab[:, 1]
        )
        add_real, add_imag = right_adjoint(part_real, part_imag, matrix[0], matrix[1])
        total_real = total_real + add_real
        total_imag = total_imag + add_imag
    partials = [jnp.stack([total_real, total_imag], axis=1)]
    stacked = jnp.stack(partials, axis=1)
    regrouped = lax.all_to_all(stacked, "energy", split_axis=3, concat_axis=0, tiled=True)
    convolved = convolve(regrouped, greater)
    returned = lax.all_to_all(convolved, "energy", split_axis=0, concat_axis=3, tiled=True)
    column = 0
    final = closing[column]
    slab_back = returned[:, column]
    mid_real, mid_imag = left_product(final[0], final[1], slab_back[:, 0], slab_back[:, 1])
    out_real, out_imag = right_adjoint(mid_real, mid_imag, final[0], final[1])
    results = [jnp.stack([out_real, out_imag], axis=1).astype(jnp.bfloat16)]
    return jnp.stack(results, axis=1)


def solution(mesh):
    placed = (
        P("energy", "space", None, None, None),
        P("space", None, None, None),
        P("space", None),
        P(None, "space", None, "energy", None),
        P("space", None, None, None),
    )
    return jax.shard_map(
        local,
        mesh=mesh,
        in_specs=placed,
        out_specs=P("energy", "space", None, None, None),
        check_vma=False,
    )
```

profile of v0, /device:TPU:0, one launch (start us, length us, event | category | flops | bytes accessed | tf_op | source)
XLA Modules:
  0.0 147.3 jit_solution(13391732195040891542)
XLA Ops:
  0.0 2.4 %collective-permute-start = (bf16[1,2,384,384]{3,2,1,0:T(8,128)(2,1)}, bf16[1,2,384,384]{3,2,1,0:T(8,128)(2,1)S(1)}, u32[]{:S(2)}, u32[]{:S(2)}) collective-permute-start(bf16[1,2,384,384]{3,2,1,0:T(8,128)(2,1)} %param.6), channel_id=1, source_target_pairs={{0,1},{2,3},{4,5},{6,7},{8,9},{10,11},{12,13},{14,15},{16,17},{18,... | collective-permute-start | bytes 1769480 | tf_op jit(solution)/shard_map/ppermute | solution.py:12
  2.4 1.3 collective-permute-start.1
  3.7 0.7 broadcast_subtract_fusion
  4.4 0.6 fusion.162
  8.9 1.4 copy.73
  12.5 0.5 fusion.46
  13.0 0.5 fusion.43
  13.5 0.5 fusion.45
  13.9 0.5 fusion.42
  14.4 0.5 fusion.44
  14.9 0.5 fusion.47
  15.3 0.5 fusion.27
  15.8 0.5 fusion.58
  16.4 0.5 fusion.25
  16.8 0.5 fusion.60
  17.4 0.5 fusion.28
  17.8 0.5 fusion.57
  18.4 0.5 fusion.26
  18.9 0.5 fusion.59
  19.4 0.5 convolution_subtract_fusion.6
  19.9 0.5 convolution_add_fusion.8
  20.5 0.5 fusion.24
  20.9 0.5 fusion.61
  21.5 0.5 convolution_subtract_fusion.5
  22.0 0.5 convolution_add_fusion.6
  22.6 0.5 fusion.29
  23.0 0.5 fusion.56
  23.6 0.5 fusion.9
  24.1 0.5 fusion.7
  24.7 0.2 maximum_bitcast_fusion
  24.9 3.4 %copy.47 = f32[2,1,2,384,384]{4,0,2,1,3:T(2,128)} copy(f32[2,1,2,384,384]{4,3,0,2,1:T(8,128)S(1)} %maximum_bitcast_fusion) | data formatting | bytes 4718592 | tf_op jit(solution)/shard_map/stack | solution.py:93
  28.3 7.8 %all-to-all-start = ((f32[2,1,2,384,384]{4,0,2,1,3:T(2,128)}), f32[2,1,2,384,384]{4,0,2,1,3:T(2,128)S(1)}, u32[]{:S(2)}, u32[]{:S(2)}) async-start(f32[2,1,2,384,384]{4,0,2,1,3:T(2,128)} %copy.47), calls=%async_computation | async-start | bytes 4718592 | tf_op jit(solution)/shard_map/all_to_all | solution.py:94
  36.1 0.1 fusion.161
  36.4 0.7 fusion.78
  37.1 0.7 fusion.74
  37.8 0.7 convolution_add_fusion.2
  38.5 1.7 %convolution_subtract_fusion.2 = f32[32,9216]{1,0:T(8,128)} fusion(f32[32,9216]{1,0:T(8,128)S(1)} %fusion.74, bf16[32,9216]{1,0:T(8,128)(2,1)S(1)} %bitcast.217), kind=kOutput, calls=%fused_computation.6 | convolution fusion | flops 113555456 | bytes 2949120 | tf_op jit(solution)/shard_map/dot_general | solution.py:36
  40.2 43.9 %all-to-all-done = f32[2,1,2,384,384]{4,0,2,1,3:T(2,128)S(1)} async-done(((f32[2,1,2,384,384]{4,0,2,1,3:T(2,128)}), f32[2,1,2,384,384]{4,0,2,1,3:T(2,128)S(1)}, u32[]{:S(2)}, u32[]{:S(2)}) %all-to-all-start) | async-done | bytes 2359328 | tf_op jit(solution)/shard_map/all_to_all | solution.py:94
  84.1 0.2 copy.48
  84.3 0.3 copy.49
  84.6 0.2 fusion.160
  84.7 0.2 copy.66
  85.0 0.2 copy.67
  85.2 1.2 fusion.76
  86.4 1.2 fusion.80
  87.6 1.2 convolution_add_fusion.1
  88.8 1.6 %multiply_subtract_fusion = (f32[32,9216]{1,0:T(8,128)S(1)}, f32[32,9216]{1,0:T(8,128)S(1)}) fusion(f32[32,9216]{1,0:T(8,128)S(1)} %copy-done.1, f32[32,9216]{1,0:T(8,128)S(1)} %convolution_add_fusion.1, f32[32,9216]{1,0:T(8,128)S(1)} %convolution_add_fusion.2, f32[32,9216]{1,0:T(8,128)S(1)} %fusion.76, f32[32,9216]{1,0:T(8,128)S(1)} %bitcast.207), kind=kOutput, calls=%fused_computation.57 | convolution fusion | flops 115324928 | bytes 8257536 | tf_op jit(solution)/shard_map/dot_general | solution.py:36
  90.4 1.2 fusion.72
  91.6 1.2 fusion.70
  92.8 1.4 fusion.2
  94.3 1.2 fusion.3
  95.6 0.1 pad_maximum_fusion
  95.8 44.6 %all_to_all.33 = bf16[32,1,2,24,384]{4,3,2,1,0:T(8,128)(2,1)S(1)} all-to-all(bf16[32,1,2,24,384]{4,3,2,1,0:T(8,128)(2,1)S(1)} %pad_maximum_fusion), channel_id=1, replica_groups=mesh['energy'=16,'space'=2] {'energy'}, dimensions={0} | all-to-all | bytes 2359296 | tf_op jit(solution)/shard_map/all_to_all | solution.py:96
  140.5 0.9 copy-done
  141.4 0.6 fusion.31
  142.0 0.6 fusion.30
  142.5 0.6 fusion.22
  143.1 0.6 fusion.36
  143.7 0.6 fusion.23
  144.3 0.6 fusion.39
  144.8 0.6 fusion.20
  145.4 0.6 fusion.21
  146.0 0.1 pad_maximum_fusion.1
  146.1 1.1 copy.59
  (17 shorter events, 0.7 us)
Async XLA Ops:
  0.0 12.2 %collective-permute-start = (bf16[1,2,384,384]{3,2,1,0:T(8,128)(2,1)}, bf16[1,2,384,384]{3,2,1,0:T(8,128)(2,1)S(1)}, u32[]{:S(2)}, u32[]{:S(2)}) collective-permute-start(bf16[1,2,384,384]{3,2,1,0:T(8,128)(2,1)} %param.6), channel_id=1, source_target_pairs={{0,1},{2,3},{4,5},{6,7},{8,9},{10,11},{12,13},{14,15},{16,17},{18,... | collective-permute-start | bytes 1769480 | tf_op jit(solution)/shard_map/ppermute | solution.py:12
  2.4 10.0 %collective-permute-start.1 = (bf16[1,2,384,384]{3,2,1,0:T(8,128)(2,1)}, bf16[1,2,384,384]{3,2,1,0:T(8,128)(2,1)S(1)}, u32[]{:S(2)}, u32[]{:S(2)}) collective-permute-start(bf16[1,2,384,384]{3,2,1,0:T(8,128)(2,1)} %param.6), channel_id=1, source_target_pairs={{1,0},{3,2},{5,4},{7,6},{9,8},{11,10},{13,12},{15,14},{17,16},{19,... | collective-permute-start | bytes 1769480 | tf_op jit(solution)/shard_map/ppermute | solution.py:12
  10.3 2.1 %copy-start.3 = (bf16[1,2,384,384]{3,2,1,0:T(8,128)(2,1)S(1)}, bf16[1,2,384,384]{3,2,1,0:T(8,128)(2,1)}, u32[]{:S(2)}) copy-start(bf16[1,2,384,384]{3,2,1,0:T(8,128)(2,1)} %param.6) | copy-start | bytes 1769476
  28.3 7.8 %copy-start.2 = (bf16[32,1,2,24,384]{4,3,2,1,0:T(8,128)(2,1)S(1)}, bf16[32,1,2,24,384]{4,3,2,1,0:T(8,128)(2,1)}, u32[]{:S(2)}) copy-start(bf16[32,1,2,24,384]{4,3,2,1,0:T(8,128)(2,1)} %param.8) | copy-start | bytes 3538948
  28.3 55.9 %all-to-all-start = ((f32[2,1,2,384,384]{4,0,2,1,3:T(2,128)}), f32[2,1,2,384,384]{4,0,2,1,3:T(2,128)S(1)}, u32[]{:S(2)}, u32[]{:S(2)}) async-start(f32[2,1,2,384,384]{4,0,2,1,3:T(2,128)} %copy.47), calls=%async_computation | async-start | bytes 4718592 | tf_op jit(solution)/shard_map/all_to_all | solution.py:94
  87.6 1.3 copy-start.1
  140.4 1.1 copy-start
where the time goes:
time: 148 us; the launch traced here: 147 us
  blocking collectives  44.6 us (30%)
  waiting for transfers between devices  43.9 us (30%)
  matrix products  30.5 us (21%)
  starting transfers between devices  11.5 us (8%)
  local copies, waits for them, and re-layouts  9.35 us (6%)
  between operations  6.3 us (4%)
    all_to_all x1, blocking collectives, local(): lax.all_to_all(convolved, 'energy', split_axis=0, concat_axis=3, tiled=True)  44.6 us
    all_to_all x1, waiting for transfers between devices, local(): lax.all_to_all(stacked, 'energy', split_axis=3, concat_axis=0, tiled=True)  43.9 us
    dot_general x12, matrix products, exact_dot(): jnp.dot(table, values, precision=lax.Precision.HIGHEST, preferred_element...  14 us
    dot_general x16, matrix products, mult(): return jnp.einsum('ers,ts->ert', a, b, preferred_element_type=jnp.float32)  8.7 us
    all_to_all x1, starting transfers between devices, local(): lax.all_to_all(stacked, 'energy', split_axis=3, concat_axis=0, tiled=True)  7.81 us
    dot_general x16, matrix products, mult(): return jnp.einsum('rs,est->ert', a, b, preferred_element_type=jnp.float32)  7.8 us
    ppermute x2, starting transfers between devices, shifted(): return lax.ppermute(block, axis, route)  3.72 us
    another operation x1, local copies, waits for them, and re-layouts, local(): stacked = jnp.stack(partials, axis=1)  3.41 us
  transfers between devices with their start and end apart: 3, of which 1 were waited for; matrix products, arithmetic and copies ran while one was open for 5% of the time, Pallas kernels for 0%

commit v1 on v0

v1 whole, which is shorter than its diff:
```python
import cmath
import functools
import math

import jax
import jax.numpy as jnp
from jax import lax
from jax.experimental import pallas as pl
from jax.experimental.pallas import tpu as pltpu
from jax.sharding import PartitionSpec as P

F32 = jnp.float32
BF16 = jnp.bfloat16


def times(value, factor):
    re, im = value
    a, b = factor.real, factor.imag
    if abs(b) < 1e-12:
        if abs(a - 1) < 1e-12:
            return value
        if abs(a + 1) < 1e-12:
            return (-re, -im)
        return (re * a, im * a)
    if abs(a) < 1e-12:
        if abs(b - 1) < 1e-12:
            return (-im, re)
        if abs(b + 1) < 1e-12:
            return (im, -re)
        return (im * -b, re * b)
    if abs(a - b) < 1e-12:
        return ((re - im) * a, (re + im) * a)
    if abs(a + b) < 1e-12:
        return ((re + im) * a, (im - re) * a)
    return (re * a - im * b, re * b + im * a)


def dft(values, sign):
    n = len(values)
    if n == 1:
        return values
    even = dft(values[0::2], sign)
    odd = dft(values[1::2], sign)
    out = [None] * n
    for k in range(n // 2):
        er, ei = even[k]
        angle = k * 4 // n if (k * 4) % n == 0 else None
        if angle == 1:
            orr, oi = odd[k]
            if sign < 0:
                out[k] = (er + oi, ei - orr)
                out[k + n // 2] = (er - oi, ei + orr)
            else:
                out[k] = (er - oi, ei + orr)
                out[k + n // 2] = (er + oi, ei - orr)
            continue
        tr, ti = times(odd[k], cmath.exp(sign * 2j * math.pi * k / n))
        out[k] = (er + tr, ei + ti)
        out[k + n // 2] = (er - tr, ei - ti)
    return out


def dot_nn(a, b):
    return lax.dot_general(a, b, (((1,), (0,)), ((), ())), preferred_element_type=F32)


def dot_nt(a, b):
    return lax.dot_general(a, b, (((1,), (1,)), ((), ())), preferred_element_type=F32)


def kernel(
    ne, ns, pts, rows, order,
    nb_ref, lesser, coupling, greater, closing, out,
    vbuf, gbuf, wbuf, nbuf, left, right, acc, abuf,
    psend, precv, ybuf, what, ssend, srecv, sfull, obuf,
    load_sem, vs_sem, vr_sem, ps_sem, pr_sem, ss_sem, sr_sem, out_sem,
):
    me = lax.axis_index("energy")
    here = lax.axis_index("space")
    each = pts // ne
    outer = 4
    inner = pts // outer
    shifts = (1,) if ns == 2 else (1, ns - 1)

    loads = [
        pltpu.make_async_copy(coupling.at[0], vbuf.at[0], load_sem.at[0]),
        pltpu.make_async_copy(lesser.at[:, 0], gbuf, load_sem.at[1]),
        pltpu.make_async_copy(greater.at[:, 0], wbuf, load_sem.at[2]),
        pltpu.make_async_copy(closing.at[0], nbuf, load_sem.at[3]),
    ]
    for load in loads:
        load.start()

    barrier = pltpu.get_barrier_semaphore()
    for k in range(1, ne):
        pl.semaphore_signal(
            barrier, inc=1, device_id={"energy": lax.rem(me + k, ne)},
            device_id_type=pl.DeviceIdType.MESH,
        )
    for shift in shifts:
        pl.semaphore_signal(
            barrier, inc=1, device_id={"space": lax.rem(here + shift, ns)},
            device_id_type=pl.DeviceIdType.MESH,
        )

    def prepare(matrix):
        re = matrix[0]
        im = matrix[1]
        left[0:order, 0:order] = re
        left[0:order, order:] = -im
        left[order:, 0:order] = im
        left[order:, order:] = re
        right[0:order, 0:order] = re
        right[0:order, order:] = im
        right[order:, 0:order] = -im
        right[order:, order:] = re

    def congruence(stacked):
        mid = dot_nn(left[...], stacked).astype(BF16)
        abuf[:, 0:order] = mid[0:order]
        abuf[:, order:] = mid[order:]
        return dot_nt(abuf[...], right[...])

    def weight(block):
        total = jnp.int32(0)
        for term in range(3):
            total = total + jnp.where(nb_ref[0, term] == block, 1, 0)
        return total.astype(F32)

    def energy_slab(e):
        return gbuf[e].reshape(2 * order, order)

    loads[0].wait()
    prepare(vbuf.at[0])
    loads[1].wait()
    own = weight(here)
    acc[0] = congruence(energy_slab(0)) * own

    pl.semaphore_wait(barrier, ne - 1 + len(shifts))
    vcopies = []
    for at, shift in enumerate(shifts):
        copy = pltpu.make_async_remote_copy(
            src_ref=coupling.at[0], dst_ref=vbuf.at[1 + at],
            send_sem=vs_sem.at[at], recv_sem=vr_sem.at[at],
            device_id={"space": lax.rem(here + shift, ns)},
            device_id_type=pl.DeviceIdType.MESH,
        )
        copy.start()
        vcopies.append(copy)
    for e in range(1, each):
        acc[e] = congruence(energy_slab(e)) * own

    pcopies = []
    for at, shift in enumerate(shifts):
        vcopies[at].wait()
        prepare(vbuf.at[1 + at])
        other = weight(lax.rem(here + ns - shift, ns))
        for e in range(each):
            total = acc[e] + congruence(energy_slab(e)) * other
            if at < len(shifts) - 1:
                acc[e] = total
                continue
            for j in range(ne):
                psend[e, j, 0] = total[j * rows:(j + 1) * rows, 0:order].astype(BF16)
                psend[e, j, 1] = total[j * rows:(j + 1) * rows, order:].astype(BF16)
            for k in range(1, ne):
                peer = lax.rem(me + k, ne)
                copy = pltpu.make_async_remote_copy(
                    src_ref=psend.at[e, peer], dst_ref=precv.at[me * each + e],
                    send_sem=ps_sem.at[e, k], recv_sem=pr_sem.at[e, k],
                    device_id={"energy": peer}, device_id_type=pl.DeviceIdType.MESH,
                )
                copy.start()
                pcopies.append(copy)
            precv[me * each + e] = psend[e, me]

    root = lambda power: cmath.exp(-2j * math.pi * power / pts)
    lanes = 128
    chunk = 8 if rows % 8 == 0 else rows

    def outer_forward(source):
        def step(c, carry):
            at = pl.ds(pl.multiple_of(c * lanes, lanes), lanes)
            for n2 in range(inner):
                taken = [
                    (source[inner * n1 + n2, 0, :, at].astype(F32),
                     source[inner * n1 + n2, 1, :, at].astype(F32))
                    for n1 in range(outer)
                ]
                for k1, value in enumerate(dft(taken, -1)):
                    re, im = times(value, root(n2 * k1))
                    ybuf[k1, n2, 0, :, at] = re
                    ybuf[k1, n2, 1, :, at] = im
            return carry

        lax.fori_loop(0, order // lanes, step, 0)

    def over_tiles(body):
        across = order // lanes

        def step(c, carry):
            at = (
                slice(None) if chunk == rows
                else pl.ds(pl.multiple_of((c // across) * chunk, chunk), chunk),
                pl.ds(pl.multiple_of((c % across) * lanes, lanes), lanes),
            )
            body(at)
            return carry

        lax.fori_loop(0, (rows // chunk) * across, step, 0)

    def screened(at):
        for k1 in range(outer):
            taken = [(ybuf[(k1, n2, 0) + at], ybuf[(k1, n2, 1) + at]) for n2 in range(inner)]
            for k2, (re, im) in enumerate(dft(taken, -1)):
                what[(k1, k2, 0) + at] = re * (1.0 / pts)
                what[(k1, k2, 1) + at] = im * (1.0 / pts)

    def middle(at):
        for k1 in range(outer):
            taken = [(ybuf[(k1, n2, 0) + at], ybuf[(k1, n2, 1) + at]) for n2 in range(inner)]
            made = []
            for k2, (re, im) in enumerate(dft(taken, -1)):
                wr = what[(k1, k2, 0) + at]
                wi = what[(k1, k2, 1) + at]
                made.append((re * wr - im * wi, re * wi + im * wr))
            for n2, value in enumerate(dft(made, 1)):
                re, im = times(value, root(-n2 * k1))
                ybuf[(k1, n2, 0) + at] = re
                ybuf[(k1, n2, 1) + at] = im

    def outer_back():
        def step(c, carry):
            at = pl.ds(pl.multiple_of(c * lanes, lanes), lanes)
            for n2 in range(inner):
                taken = [
                    (ybuf[k1, n2, 0, :, at], ybuf[k1, n2, 1, :, at]) for k1 in range(outer)
                ]
                for n1, (re, im) in enumerate(dft(taken, 1)):
                    ssend[inner * n1 + n2, 0, :, at] = re.astype(BF16)
                    ssend[inner * n1 + n2, 1, :, at] = im.astype(BF16)
            return carry

        lax.fori_loop(0, order // lanes, step, 0)

    loads[2].wait()
    outer_forward(wbuf)
    over_tiles(screened)
    loads[3].wait()
    prepare(nbuf)

    for copy in pcopies:
        copy.wait_recv()
    outer_forward(precv)
    over_tiles(middle)
    outer_back()

    scopies = []
    for e in range(each):
        for k in range(1, ne):
            peer = lax.rem(me + k, ne)
            copy = pltpu.make_async_remote_copy(
                src_ref=ssend.at[peer * each + e], dst_ref=srecv.at[e, me],
                send_sem=ss_sem.at[e, k], recv_sem=sr_sem.at[e, k],
                device_id={"energy": peer}, device_id_type=pl.DeviceIdType.MESH,
            )
            copy.start()
            scopies.append(copy)
        srecv[e, me] = ssend[me * each + e]

    for copy in pcopies:
        copy.wait_send()

    stores = []
    for e in range(each):
        for copy in scopies[e * (ne - 1):(e + 1) * (ne - 1)]:
            copy.wait_recv()
        for j in range(ne):
            for part in range(2):
                sfull[part * order + j * rows:part * order + (j + 1) * rows, :] = (
                    srecv[e, j, part].astype(F32)
                )
        result = congruence(sfull[...].astype(BF16)).astype(BF16)
        obuf[e, 0] = result[:, 0:order]
        obuf[e, 1] = result[:, order:]
        store = pltpu.make_async_copy(obuf.at[e], out.at[e, 0], out_sem.at[e])
        store.start()
        stores.append(store)
    for copy in scopies:
        copy.wait_send()
    for store in stores:
        store.wait()


def local(ne, ns, lesser, coupling, neighbours, greater, closing):
    each = lesser.shape[0]
    pts = greater.shape[0]
    rows, order = greater.shape[3], greater.shape[4]
    outer = 4
    cands = 1 if ns == 2 else 2
    anywhere = pl.BlockSpec(memory_space=pl.ANY)
    dma = pltpu.SemaphoreType.DMA
    return pl.pallas_call(
        functools.partial(kernel, ne, ns, pts, rows, order),
        out_shape=jax.ShapeDtypeStruct(lesser.shape, BF16),
        in_specs=[pl.BlockSpec(memory_space=pltpu.SMEM)] + [anywhere] * 4,
        out_specs=anywhere,
        scratch_shapes=[
            pltpu.VMEM((1 + cands, 2, order, order), BF16),
            pltpu.VMEM((each, 2, order, order), BF16),
            pltpu.VMEM((pts, 2, rows, order), BF16),
            pltpu.VMEM((2, order, order), BF16),
            pltpu.VMEM((2 * order, 2 * order), BF16),
            pltpu.VMEM((2 * order, 2 * order), BF16),
            pltpu.VMEM((each, order, 2 * order), F32),
            pltpu.VMEM((order, 2 * order), BF16),
            pltpu.VMEM((each, ne, 2, rows, order), BF16),
            pltpu.VMEM((pts, 2, rows, order), BF16),
            pltpu.VMEM((outer, pts // outer, 2, rows, order), F32),
            pltpu.VMEM((outer, pts // outer, 2, rows, order), F32),
            pltpu.VMEM((pts, 2, rows, order), BF16),
            pltpu.VMEM((each, ne, 2, rows, order), BF16),
            pltpu.VMEM((2 * order, order), F32),
            pltpu.VMEM((each, 2, order, order), BF16),
            dma((4,)), dma((cands,)), dma((cands,)),
            dma((each, ne)), dma((each, ne)), dma((each, ne)), dma((each, ne)),
            dma((each,)),
        ],
        compiler_params=pltpu.CompilerParams(
            collective_id=0, has_side_effects=True, vmem_limit_bytes=60 * 1024 * 1024
        ),
    )(neighbours, lesser, coupling, greater, closing)


def solution(mesh):
    placed = (
        P("energy", "space", None, None, None),
        P("space", None, None, None),
        P("space", None),
        P(None, "space", None, "energy", None),
        P("space", None, None, None),
    )
    return jax.shard_map(
        functools.partial(local, mesh.shape["energy"], mesh.shape["space"]),
        mesh=mesh,
        in_specs=placed,
        out_specs=P("energy", "space", None, None, None),
        check_vma=False,
    )
```

time: 148 us -> 69.9 us (0.47)
  the two profiles are of different devices: /device:TPU:0 before, /device:TPU:28 now
where the time goes in v1:
time: 69.9 us; the launch traced here: 69.7 us
  Pallas kernels  67.3 us (96%)
  local copies, waits for them, and re-layouts  2.4 us (3%)
    pallas_call x1, Pallas kernels, local(): pl.pallas_call(functools.partial(kernel, ne, ns, pts, rows, order), out_s...  67.3 us
    unnamed x1, local copies, waits for them, and re-layouts  2.4 us

profile of v1, /device:TPU:28, one launch (start us, length us, event | category | flops | bytes accessed | tf_op | source)
XLA Modules:
  0.0 69.7 jit_solution(14161712791488051448)
XLA Ops:
  0.0 67.3 %shard_map.55 = bf16[2,1,2,384,384]{4,3,2,1,0:T(8,128)(2,1)} custom-call(s32[1,3]{1,0:T(1,128)} %nb_ref.1, bf16[2,1,2,384,384]{4,3,2,1,0:T(8,128)(2,1)} %lesser.1, bf16[1,2,384,384]{3,2,1,0:T(8,128)(2,1)} %coupling.1, bf16[32,1,2,24,384]{4,3,2,1,0:T(8,128)(2,1)} %greater.1, bf16[1,2,384,384]{3,2,1,0:T(8,128)(2,1)} %closing.1), custom_call_target="tpu_custom_call" | custom-call | tf_op jit(solution)/shard_map/pallas_call | solution.py:303
  67.3 2.4 %copy.7 = bf16[2,1,2,384,384]{4,3,2,1,0:T(8,128)(2,1)} copy(bf16[2,1,2,384,384]{4,3,2,1,0:T(8,128)(2,1)} %shard_map.55) | data formatting | bytes 2359296

commit v2 on v1

v2 whole, which is shorter than its diff:
```python
import cmath
import functools
import math

import jax
import jax.numpy as jnp
from jax import lax
from jax.experimental import pallas as pl
from jax.experimental.pallas import tpu as pltpu
from jax.sharding import PartitionSpec as P

F32 = jnp.float32
BF16 = jnp.bfloat16
VMEM_LIMIT = 48 * 1024 * 1024


def times(value, factor):
    re, im = value
    a, b = factor.real, factor.imag
    if abs(b) < 1e-12:
        if abs(a - 1) < 1e-12:
            return value
        if abs(a + 1) < 1e-12:
            return (-re, -im)
        return (re * a, im * a)
    if abs(a) < 1e-12:
        if abs(b - 1) < 1e-12:
            return (-im, re)
        if abs(b + 1) < 1e-12:
            return (im, -re)
        return (im * -b, re * b)
    if abs(a - b) < 1e-12:
        return ((re - im) * a, (re + im) * a)
    if abs(a + b) < 1e-12:
        return ((re + im) * a, (im - re) * a)
    return (re * a - im * b, re * b + im * a)


def dft(values, sign):
    n = len(values)
    if n == 1:
        return values
    even = dft(values[0::2], sign)
    odd = dft(values[1::2], sign)
    out = [None] * n
    for k in range(n // 2):
        er, ei = even[k]
        angle = k * 4 // n if (k * 4) % n == 0 else None
        if angle == 1:
            orr, oi = odd[k]
            if sign < 0:
                out[k] = (er + oi, ei - orr)
                out[k + n // 2] = (er - oi, ei + orr)
            else:
                out[k] = (er - oi, ei + orr)
                out[k + n // 2] = (er + oi, ei - orr)
            continue
        tr, ti = times(odd[k], cmath.exp(sign * 2j * math.pi * k / n))
        out[k] = (er + tr, ei + ti)
        out[k + n // 2] = (er - tr, ei - ti)
    return out


def dot_nn(a, b):
    return lax.dot_general(a, b, (((1,), (0,)), ((), ())), preferred_element_type=F32)


def dot_nt(a, b):
    return lax.dot_general(a, b, (((1,), (1,)), ((), ())), preferred_element_type=F32)


def kernel(
    ne, ns, pts, rows, order, widths,
    nb_ref, lesser, coupling, greater, closing, out,
    vbuf, gbuf, wbuf, nbuf, gemb, acc, abuf, ybuf, what, sfull, semb, obuf,
    psend, precv, ssend, srecv,
    load_sem, vs_sem, vr_sem, ps_sem, pr_sem, ss_sem, sr_sem, out_sem,
):
    me = lax.axis_index("energy")
    here = lax.axis_index("space")
    each = pts // ne
    outer = 4
    inner = pts // outer
    shifts = (1,) if ns == 2 else (1, ns - 1)
    starts = [sum(widths[:c]) for c in range(len(widths))]
    chunks = range(len(widths))

    loads = [
        pltpu.make_async_copy(lesser.at[:, 0], gbuf, load_sem.at[0]),
        pltpu.make_async_copy(coupling.at[0, 0], vbuf.at[0, :, 0:order], load_sem.at[1]),
        pltpu.make_async_copy(coupling.at[0, 1], vbuf.at[0, :, order:], load_sem.at[2]),
        pltpu.make_async_copy(greater.at[:, 0], wbuf, load_sem.at[3]),
        pltpu.make_async_copy(closing.at[0, 0], nbuf.at[:, 0:order], load_sem.at[4]),
        pltpu.make_async_copy(closing.at[0, 1], nbuf.at[:, order:], load_sem.at[5]),
    ]
    for load in loads:
        load.start()

    barrier = pltpu.get_barrier_semaphore()
    for k in range(1, ne):
        pl.semaphore_signal(
            barrier, inc=1, device_id={"energy": lax.rem(me + k, ne)},
            device_id_type=pl.DeviceIdType.MESH,
        )
    for shift in shifts:
        pl.semaphore_signal(
            barrier, inc=1, device_id={"space": lax.rem(here + shift, ns)},
            device_id_type=pl.DeviceIdType.MESH,
        )

    def embed(e):
        re = gbuf[e, 0]
        im = gbuf[e, 1]
        gemb[e, 0:order, 0:order] = re
        gemb[e, 0:order, order:] = im
        gemb[e, order:, 0:order] = -im
        gemb[e, order:, order:] = re

    def place(slot, re, im, start, width):
        at = slice(start, start + width)
        to = slice(order + start, order + start + width)
        abuf[slot, 0:order, at] = re
        abuf[slot, 0:order, to] = im
        abuf[slot, order:, at] = im
        abuf[slot, order:, to] = -re

    def left(slot, e, at):
        mid = dot_nn(vbuf[at], gemb[e]).astype(BF16)
        place(slot, mid[:, 0:order], mid[:, order:], 0, order)

    def weight(block):
        total = jnp.int32(0)
        for term in range(3):
            total = total + jnp.where(nb_ref[0, term] == block, 1, 0)
        return total.astype(F32)

    def own_term(e):
        left(0, e, 0)
        acc[e] = dot_nt(abuf[0], vbuf[0]) * own

    own = weight(here)
    loads[0].wait()
    embed(0)
    loads[1].wait()
    loads[2].wait()
    own_term(0)
    for e in range(1, each):
        embed(e)

    pl.semaphore_wait(barrier, ne - 1 + len(shifts))
    vcopies = []
    for at, shift in enumerate(shifts):
        for part in range(2):
            copy = pltpu.make_async_remote_copy(
                src_ref=coupling.at[0, part],
                dst_ref=vbuf.at[1 + at, :, part * order:(part + 1) * order],
                send_sem=vs_sem.at[at, part], recv_sem=vr_sem.at[at, part],
                device_id={"space": lax.rem(here + shift, ns)},
                device_id_type=pl.DeviceIdType.MESH,
            )
            copy.start()
            vcopies.append(copy)
    for e in range(1, each):
        own_term(e)
    for copy in vcopies:
        copy.wait()
    others = [weight(lax.rem(here + ns - shift, ns)) for shift in shifts]
    for at in range(len(shifts) - 1):
        for e in range(each):
            left(0, e, 1 + at)
            acc[e] = acc[e] + dot_nt(abuf[0], vbuf[1 + at]) * others[at]
    last = len(shifts)

    def last_term(e, c):
        span = slice(starts[c], starts[c] + widths[c])
        total = acc[e, :, span] + dot_nt(abuf[e], vbuf[last, span]) * others[-1]
        for j in range(ne):
            for part in range(2):
                psend[c][e, j, part] = total[
                    part * order + j * rows:part * order + (j + 1) * rows
                ].astype(BF16)

    pcopies = [[] for _ in chunks]

    def send_p(e, c):
        for k in range(1, ne):
            peer = lax.rem(me + k, ne)
            copy = pltpu.make_async_remote_copy(
                src_ref=psend[c].at[e, peer], dst_ref=precv[c].at[me * each + e],
                send_sem=ps_sem.at[c, e, k], recv_sem=pr_sem.at[c, e, k],
                device_id={"energy": peer}, device_id_type=pl.DeviceIdType.MESH,
            )
            copy.start()
            pcopies[c].append(copy)
        precv[c][me * each + e] = psend[c][e, me]

    for c in chunks:
        for e in range(each):
            if c == 0:
                left(e, e, last)
            last_term(e, c)
            send_p(e, c)

    root = lambda power: cmath.exp(-2j * math.pi * power / pts)
    lanes = 128
    chunk = 8 if rows % 8 == 0 else rows

    def lane_tiles(start, width, body):
        def step(c, carry):
            body(
                pl.ds(pl.multiple_of(start + c * lanes, lanes), lanes),
                pl.ds(pl.multiple_of(c * lanes, lanes), lanes),
            )
            return carry

        lax.fori_loop(0, width // lanes, step, 0)

    def outer_forward(source, start, width):
        def body(at, near):
            for n2 in range(inner):
                taken = [
                    (source[inner * n1 + n2, 0, :, near].astype(F32),
                     source[inner * n1 + n2, 1, :, near].astype(F32))
                    for n1 in range(outer)
                ]
                for k1, value in enumerate(dft(taken, -1)):
                    re, im = times(value, root(n2 * k1))
                    ybuf[k1, n2, 0, :, at] = re
                    ybuf[k1, n2, 1, :, at] = im

        lane_tiles(start, width, body)

    def over_tiles(start, width, body):
        across = width // lanes

        def step(c, carry):
            at = (
                slice(None) if chunk == rows
                else pl.ds(pl.multiple_of((c // across) * chunk, chunk), chunk),
                pl.ds(pl.multiple_of(start + (c % across) * lanes, lanes), lanes),
            )
            body(at)
            return carry

        lax.fori_loop(0, (rows // chunk) * across, step, 0)

    def screened(at):
        for k1 in range(outer):
            taken = [(ybuf[(k1, n2, 0) + at], ybuf[(k1, n2, 1) + at]) for n2 in range(inner)]
            for k2, (re, im) in enumerate(dft(taken, -1)):
                what[(k1, k2, 0) + at] = re * (1.0 / pts)
                what[(k1, k2, 1) + at] = im * (1.0 / pts)

    def middle(at):
        for k1 in range(outer):
            taken = [(ybuf[(k1, n2, 0) + at], ybuf[(k1, n2, 1) + at]) for n2 in range(inner)]
            made = []
            for k2, (re, im) in enumerate(dft(taken, -1)):
                wr = what[(k1, k2, 0) + at]
                wi = what[(k1, k2, 1) + at]
                made.append((re * wr - im * wi, re * wi + im * wr))
            for n2, value in enumerate(dft(made, 1)):
                re, im = times(value, root(-n2 * k1))
                ybuf[(k1, n2, 0) + at] = re
                ybuf[(k1, n2, 1) + at] = im

    def outer_back(target, start, width):
        def body(at, near):
            for n2 in range(inner):
                taken = [
                    (ybuf[k1, n2, 0, :, at], ybuf[k1, n2, 1, :, at]) for k1 in range(outer)
                ]
                for n1, (re, im) in enumerate(dft(taken, 1)):
                    target[inner * n1 + n2, 0, :, near] = re.astype(BF16)
                    target[inner * n1 + n2, 1, :, near] = im.astype(BF16)

        lane_tiles(start, width, body)

    loads[3].wait()
    outer_forward(wbuf, 0, order)
    over_tiles(0, order, screened)
    loads[4].wait()
    loads[5].wait()

    scopies = {}
    for c in chunks:
        for copy in pcopies[c]:
            copy.wait_recv()
        outer_forward(precv[c], starts[c], widths[c])
        over_tiles(starts[c], widths[c], middle)
        outer_back(ssend[c], starts[c], widths[c])
        for e in range(each):
            scopies[c, e] = []
            for k in range(1, ne):
                peer = lax.rem(me + k, ne)
                copy = pltpu.make_async_remote_copy(
                    src_ref=ssend[c].at[peer * each + e], dst_ref=srecv[c].at[e, me],
                    send_sem=ss_sem.at[c, e, k], recv_sem=sr_sem.at[c, e, k],
                    device_id={"energy": peer}, device_id_type=pl.DeviceIdType.MESH,
                )
                copy.start()
                scopies[c, e].append(copy)
            srecv[c][e, me] = ssend[c][me * each + e]

    stores = []
    for c in chunks:
        width = widths[c]
        for e in range(each):
            for copy in scopies[c, e]:
                copy.wait_recv()
            for j in range(ne):
                for part in range(2):
                    sfull[part, j * rows:(j + 1) * rows, 0:width] = (
                        srecv[c][e, j, part].astype(F32)
                    )
            re = sfull[0, :, 0:width].astype(BF16)
            im = sfull[1, :, 0:width].astype(BF16)
            semb[0:order, 0:width] = re
            semb[0:order, width:2 * width] = im
            semb[order:, 0:width] = -im
            semb[order:, width:2 * width] = re
            mid = dot_nn(nbuf[...], semb[:, 0:2 * width]).astype(BF16)
            place(e, mid[:, 0:width], mid[:, width:], starts[c], width)
            if c < len(widths) - 1:
                continue
            result = dot_nt(abuf[e], nbuf[...]).astype(BF16)
            obuf[e, 0] = result[0:order]
            obuf[e, 1] = result[order:]
            store = pltpu.make_async_copy(obuf.at[e], out.at[e, 0], out_sem.at[e])
            store.start()
            stores.append(store)
    for c in chunks:
        for copy in pcopies[c]:
            copy.wait_send()
        for e in range(each):
            for copy in scopies[c, e]:
                copy.wait_send()
    for store in stores:
        store.wait()


def local(ne, ns, lesser, coupling, neighbours, greater, closing):
    each = lesser.shape[0]
    pts = greater.shape[0]
    rows, order = greater.shape[3], greater.shape[4]
    outer = 4
    cands = 1 if ns == 2 else 2
    tail = max(1, order // 128 // 3) * 128
    widths = (order - tail, tail)
    resident = pl.BlockSpec(memory_space=pltpu.HBM)
    dma = pltpu.SemaphoreType.DMA
    spread = [pltpu.VMEM((each, ne, 2, rows, width), BF16) for width in widths]
    whole = [pltpu.VMEM((pts, 2, rows, width), BF16) for width in widths]
    counts = dma((len(widths), each, ne))
    return pl.pallas_call(
        functools.partial(kernel, ne, ns, pts, rows, order, widths),
        out_shape=jax.ShapeDtypeStruct(lesser.shape, BF16),
        in_specs=[pl.BlockSpec(memory_space=pltpu.SMEM)] + [resident] * 4,
        out_specs=pl.BlockSpec(memory_space=pl.ANY),
        scratch_shapes=[
            pltpu.VMEM((1 + cands, order, 2 * order), BF16),
            pltpu.VMEM((each, 2, order, order), BF16),
            pltpu.VMEM((pts, 2, rows, order), BF16),
            pltpu.VMEM((order, 2 * order), BF16),
            pltpu.VMEM((each, 2 * order, 2 * order), BF16),
            pltpu.VMEM((each, 2 * order, order), F32),
            pltpu.VMEM((each, 2 * order, 2 * order), BF16),
            pltpu.VMEM((outer, pts // outer, 2, rows, order), F32),
            pltpu.VMEM((outer, pts // outer, 2, rows, order), F32),
            pltpu.VMEM((2, order, widths[0]), F32),
            pltpu.VMEM((2 * order, 2 * widths[0]), BF16),
            pltpu.VMEM((each, 2, order, order), BF16),
            spread, whole, whole, spread,
            dma((6,)), dma((cands, 2)), dma((cands, 2)),
            counts, counts, counts, counts,
            dma((each,)),
        ],
        compiler_params=pltpu.CompilerParams(
            collective_id=0, has_side_effects=True, vmem_limit_bytes=VMEM_LIMIT
        ),
    )(*(
        pltpu.with_memory_space_constraint(x, pltpu.HBM)
        for x in (neighbours, lesser, coupling, greater, closing)
    ))


def solution(mesh):
    placed = (
        P("energy", "space", None, None, None),
        P("space", None, None, None),
        P("space", None),
        P(None, "space", None, "energy", None),
        P("space", None, None, None),
    )
    return jax.shard_map(
        functools.partial(local, mesh.shape["energy"], mesh.shape["space"]),
        mesh=mesh,
        in_specs=placed,
        out_specs=P("energy", "space", None, None, None),
        check_vma=False,
    )
```

time: 69.9 us -> 68 us (0.973)
  the two profiles are of different devices: /device:TPU:28 before, /device:TPU:0 now
where the time goes in v2:
time: 68 us; the launch traced here: 67.8 us
  Pallas kernels  66.8 us (98%)
  local copies, waits for them, and re-layouts  1.02 us (2%)
    pallas_call x1, Pallas kernels, local(): pl.pallas_call(functools.partial(kernel, ne, ns, pts, rows, order, widths...  66.8 us

profile of v2, /device:TPU:0, one launch (start us, length us, event | category | flops | bytes accessed | tf_op | source)
XLA Modules:
  0.0 67.8 jit_solution(13095637446111757074)
XLA Ops:
  0.0 66.8 %shard_map.55 = bf16[2,1,2,384,384]{4,3,2,1,0:T(8,128)(2,1)S(1)} custom-call(s32[1,3]{1,0:T(1,128)} %nb_ref.1, bf16[2,1,2,384,384]{4,3,2,1,0:T(8,128)(2,1)} %lesser.1, bf16[1,2,384,384]{3,2,1,0:T(8,128)(2,1)} %coupling.1, bf16[32,1,2,24,384]{4,3,2,1,0:T(8,128)(2,1)} %greater.1, bf16[1,2,384,384]{3,2,1,0:T(8,128)(2,1)} %closing.1), custom_call_target="tpu_custom_call" | custom-call | tf_op jit(solution)/shard_map/pallas_call | solution.py:355
  66.8 1.0 %copy.7 = bf16[2,1,2,384,384]{4,3,2,1,0:T(8,128)(2,1)} copy(bf16[2,1,2,384,384]{4,3,2,1,0:T(8,128)(2,1)S(1)} %shard_map.55) | data formatting | bytes 2359296

commit v3 on v2

--- a/solution.py
+++ b/solution.py
@@ -82,6 +82,9 @@
     outer = 4
     inner = pts // outer
     shifts = (1,) if ns == 2 else (1, ns - 1)
+    half = ne // 2
+    side = me // half
+    peers = [lax.rem(me + k, ne) for k in range(1, ne)]
     starts = [sum(widths[:c]) for c in range(len(widths))]
     chunks = range(len(widths))
 
@@ -97,9 +100,9 @@
         load.start()
 
     barrier = pltpu.get_barrier_semaphore()
-    for k in range(1, ne):
+    for peer in peers:
         pl.semaphore_signal(
-            barrier, inc=1, device_id={"energy": lax.rem(me + k, ne)},
+            barrier, inc=1, device_id={"energy": peer},
             device_id_type=pl.DeviceIdType.MESH,
         )
     for shift in shifts:
@@ -135,17 +138,14 @@
         return total.astype(F32)
 
     def own_term(e):
-        left(0, e, 0)
-        acc[e] = dot_nt(abuf[0], vbuf[0]) * own
+        left(e, e, 0)
+        acc[e] = dot_nt(abuf[e], vbuf[0]) * own
 
     own = weight(here)
     loads[0].wait()
     embed(0)
     loads[1].wait()
     loads[2].wait()
-    own_term(0)
-    for e in range(1, each):
-        embed(e)
 
     pl.semaphore_wait(barrier, ne - 1 + len(shifts))
     vcopies = []
@@ -160,7 +160,10 @@
             )
             copy.start()
             vcopies.append(copy)
-    for e in range(1, each):
+    ahead = 1 if len(shifts) == 1 else each
+    for e in range(1, ahead):
+        embed(e)
+    for e in range(ahead):
         own_term(e)
     for copy in vcopies:
         copy.wait()
@@ -183,8 +186,7 @@
     pcopies = [[] for _ in chunks]
 
     def send_p(e, c):
-        for k in range(1, ne):
-            peer = lax.rem(me + k, ne)
+        for k, peer in enumerate(peers):
             copy = pltpu.make_async_remote_copy(
                 src_ref=psend[c].at[e, peer], dst_ref=precv[c].at[me * each + e],
                 send_sem=ps_sem.at[c, e, k], recv_sem=pr_sem.at[c, e, k],
@@ -197,6 +199,9 @@
     for c in chunks:
         for e in range(each):
             if c == 0:
+                if e >= ahead:
+                    embed(e)
+                    own_term(e)
                 left(e, e, last)
             last_term(e, c)
             send_p(e, c)
@@ -291,8 +296,7 @@
         outer_back(ssend[c], starts[c], widths[c])
         for e in range(each):
             scopies[c, e] = []
-            for k in range(1, ne):
-                peer = lax.rem(me + k, ne)
+            for k, peer in enumerate(peers):
                 copy = pltpu.make_async_remote_copy(
                     src_ref=ssend[c].at[peer * each + e], dst_ref=srecv[c].at[e, me],
                     send_sem=ss_sem.at[c, e, k], recv_sem=sr_sem.at[c, e, k],
@@ -321,9 +325,15 @@
             semb[order:, width:2 * width] = re
             mid = dot_nn(nbuf[...], semb[:, 0:2 * width]).astype(BF16)
             place(e, mid[:, 0:width], mid[:, width:], starts[c], width)
+            span = slice(starts[c], starts[c] + width)
+            also = slice(order + starts[c], order + starts[c] + width)
+            result = dot_nt(abuf[e, :, span], nbuf[:, span]) + dot_nt(abuf[e, :, also], nbuf[:, also])
+            if c > 0:
+                result = result + acc[e]
             if c < len(widths) - 1:
+                acc[e] = result
                 continue
-            result = dot_nt(abuf[e], nbuf[...]).astype(BF16)
+            result = result.astype(BF16)
             obuf[e, 0] = result[0:order]
             obuf[e, 1] = result[order:]
             store = pltpu.make_async_copy(obuf.at[e], out.at[e, 0], out_sem.at[e])

time: 68 us -> 66.7 us (0.981)
  Pallas kernels: 66.8 us -> 65.5 us
    pallas_call x1, Pallas kernels: 66.8 us -> 65.5 us  [local(): pl.pallas_call(functools.partial(kernel, ne, ns, pts, rows, order, widths...]
where the time goes in v3:
time: 66.7 us; the launch traced here: 66.6 us
  Pallas kernels  65.5 us (98%)
  local copies, waits for them, and re-layouts  1.02 us (2%)
    pallas_call x1, Pallas kernels, local(): pl.pallas_call(functools.partial(kernel, ne, ns, pts, rows, order, widths...  65.5 us

profile of v3, /device:TPU:0, one launch (start us, length us, event | category | flops | bytes accessed | tf_op | source)
XLA Modules:
  0.0 66.6 jit_solution(16841191292063626358)
XLA Ops:
  0.0 65.5 %shard_map.55 = bf16[2,1,2,384,384]{4,3,2,1,0:T(8,128)(2,1)S(1)} custom-call(s32[1,3]{1,0:T(1,128)} %nb_ref.1, bf16[2,1,2,384,384]{4,3,2,1,0:T(8,128)(2,1)} %lesser.1, bf16[1,2,384,384]{3,2,1,0:T(8,128)(2,1)} %coupling.1, bf16[32,1,2,24,384]{4,3,2,1,0:T(8,128)(2,1)} %greater.1, bf16[1,2,384,384]{3,2,1,0:T(8,128)(2,1)} %closing.1), custom_call_target="tpu_custom_call" | custom-call | tf_op jit(solution)/shard_map/pallas_call | solution.py:365
  65.5 1.0 %copy.7 = bf16[2,1,2,384,384]{4,3,2,1,0:T(8,128)(2,1)} copy(bf16[2,1,2,384,384]{4,3,2,1,0:T(8,128)(2,1)S(1)} %shard_map.55) | data formatting | bytes 2359296
